TPU v7x, 32 devices: a whole 2x2x4 slice. The times are simulated.
32 devices in a mesh: sx: 4 (over y, x), sy: 2 (over core), op: 4 (over z).
Axes of the slice: x: 2, y: 2, z: 4, core: 2. Of those that a mesh axis runs over, the one named last changes fastest.
Arguments:
- op_real: float32 [4, 2, 6144, 6144], P('sx', 'sy', 'op'), may hold values from -0.0546875 to 0.0546875
- op_imag: float32 [4, 2, 6144, 6144], P('sx', 'sy', 'op'), may hold values from -0.0546875 to 0.0546875
- coef_right: float32 [4, 2, 2, 6144], P('sx', 'sy', None, 'op'), may hold values from -3 to 3
- coef_upper: float32 [4, 2, 2, 6144], P('sx', 'sy', None, 'op'), may hold values from -3 to 3
- sources: float32 [4, 2, 2, 16, 6144], P('sx', 'sy', None, None, 'op'), may hold values from -6 to 6
Outputs:
- traces: float32 [4, 2, 2, 16, 6144], P('sx', 'sy', None, None, 'op')
All inputs are finite; a program needn't handle non-finite values.
Results may differ from a plain program's by a relative error of at most 0.0003.
Values sent between devices are 32-bit elements; how exact they have to be, the bound alone decides.
A program may use at most 128 MiB of HBM per device.

v0:
```python
import functools

import jax
import jax.numpy as jnp
from jax import lax
from jax.experimental import pallas as pl
from jax.experimental.pallas import tpu as pltpu
from jax.sharding import PartitionSpec as P

MESH = pl.DeviceIdType.MESH
LOAD_ROWS = 32
SLOTS = 3
LOW_SCALE = 2.0**20
F8 = jnp.float8_e4m3fn
F32 = jnp.float32
BF16 = jnp.bfloat16
NT = (((1,), (1,)), ((), ()))


def kernel(
    ncol, nrow, nop, groups, block,
    real_hbm, imag_hbm, right_ref, upper_ref, src_ref, out_ref,
    high, low, stage, gathered, xw, x8, inv, left_buf, below_buf, trace,
    load_sem, gsend, grecv, lsend, lrecv, usend, urecv,
):
    c = lax.axis_index("sx")
    r = lax.axis_index("sy")
    z = lax.axis_index("op")
    first = c + r == 0
    rows, width = real_hbm.shape
    srcs = src_ref.shape[1]
    group_rows = rows // groups
    chunks = rows // LOAD_ROWS
    per_block = block // LOAD_ROWS
    blocks = group_rows // block
    ops = (real_hbm, imag_hbm)

    def load(chunk, slot, k):
        at = pl.multiple_of(chunk * LOAD_ROWS, LOAD_ROWS)
        return pltpu.make_async_copy(
            ops[k].at[pl.ds(at, LOAD_ROWS), :], stage.at[slot, k], load_sem.at[slot, k]
        )

    for s in range(SLOTS):
        for k in range(2):
            load(s, s, k).start()

    barrier = pltpu.get_barrier_semaphore()
    for j in range(1, nop):
        pl.semaphore_signal(
            barrier, inc=1, device_id=(c, r, lax.rem(z + j, nop)), device_id_type=MESH
        )

    def greet(cond, cc, rr):
        @pl.when(cond)
        def _():
            pl.semaphore_signal(barrier, inc=1, device_id=(cc, rr, z), device_id_type=MESH)

    has_left, has_right = c > 0, c < ncol - 1
    has_below, has_above = r > 0, r < nrow - 1
    greet(has_left, c - 1, r)
    greet(has_right, c + 1, r)
    greet(has_below, c, r - 1)
    greet(has_above, c, r + 1)
    near = sum(jnp.where(cond, 1, 0) for cond in (has_left, has_right, has_below, has_above))
    pl.semaphore_wait(barrier, nop - 1 + near)

    def send_right(g):
        return pltpu.make_async_remote_copy(
            trace.at[g], left_buf.at[g], lsend.at[g], lrecv.at[g],
            device_id=(c + 1, r, z), device_id_type=MESH,
        )

    def send_up(g):
        return pltpu.make_async_remote_copy(
            trace.at[g], below_buf.at[g], usend.at[g], urecv.at[g],
            device_id=(c, r + 1, z), device_id_type=MESH,
        )

    def share(g, j):
        peer = lax.rem(z + j, nop)
        return pltpu.make_async_remote_copy(
            gathered.at[z, g], gathered.at[z, g], gsend.at[g, j], grecv.at[g, j],
            device_id=(c, r, peer), device_id_type=MESH,
        )

    def gather():
        for g in range(groups):
            cols = pl.ds(g * group_rows, group_rows)
            gathered[z, g] = src_ref[:, :, cols]

            def add(coef_ref, buf):
                cr = coef_ref[0:1, cols]
                ci = coef_ref[1:2, cols]
                gathered[z, g, 0] += cr * buf[g, 0] - ci * buf[g, 1]
                gathered[z, g, 1] += cr * buf[g, 1] + ci * buf[g, 0]

            @pl.when(has_left)
            def _():
                send_right(g).wait_recv()
                add(right_ref, left_buf)

            @pl.when(has_below)
            def _():
                send_up(g).wait_recv()
                add(upper_ref, below_buf)

            for j in range(1, nop):
                share(g, j).start()
        for g in range(groups):
            for j in range(1, nop):
                share(g, j).wait()

        def largest(step, top):
            zz, g = step // groups, lax.rem(step, groups)
            both = jnp.maximum(jnp.abs(gathered[zz, g, 0]), jnp.abs(gathered[zz, g, 1]))
            return jnp.maximum(top, jnp.max(both, axis=1, keepdims=True))

        top = lax.fori_loop(0, nop * groups, largest, jnp.zeros((srcs, 1), F32))
        top = jnp.maximum(top, 1e-30)
        inv[...] = jnp.broadcast_to(top * (1.0 / (256.0 * LOW_SCALE)), inv.shape)
        scale = 256.0 / top

        @pl.loop(0, nop * groups)
        def _(step):
            zz, g = step // groups, lax.rem(step, groups)
            at = pl.multiple_of(step * group_rows, group_rows)
            for k in range(2):
                value = gathered[zz, g, k]
                top_part = value.astype(BF16)
                xw[k * srcs:(k + 1) * srcs, pl.ds(at, group_rows)] = top_part
                xw[(2 + k) * srcs:(3 + k) * srcs, pl.ds(at, group_rows)] = (
                    value - top_part.astype(F32)
                ).astype(BF16)
            both = jnp.concatenate([gathered[zz, g, 0] * scale, gathered[zz, g, 1] * scale], axis=0)
            x8[:, pl.ds(at, group_rows)] = both.astype(F8)

    def convert(b):
        @pl.loop(0, per_block)
        def _(i):
            chunk = b * per_block + i
            slot = lax.rem(chunk, SLOTS)
            at = pl.multiple_of(chunk * LOAD_ROWS, LOAD_ROWS)
            for k in range(2):
                load(chunk, slot, k).wait()

                @pl.loop(0, width // 512)
                def _(q):
                    cols = pl.ds(pl.multiple_of(q * 512, 512), 512)
                    value = stage[slot, k, :, cols]
                    top_part = value.astype(BF16)
                    high[k, pl.ds(at, LOAD_ROWS), cols] = top_part
                    low[k, pl.ds(at, LOAD_ROWS), cols] = (
                        (value - top_part.astype(F32)) * LOW_SCALE
                    ).astype(F8)

            @pl.when(chunk + SLOTS < chunks)
            def _():
                for k in range(2):
                    load(chunk + SLOTS, slot, k).start()

    def multiply(g, b):
        at = pl.ds(pl.multiple_of((g * blocks + b) * block, block), block)
        here = pl.ds(pl.multiple_of(b * block, block), block)
        parts = []
        for k in range(2):
            big = lax.dot_general(high[k, at, :], xw[...], NT, preferred_element_type=F32).T
            small = lax.dot_general(low[k, at, :], x8[...], NT, preferred_element_type=F32).T
            factor = jnp.concatenate([inv[:, :1], inv[:, :1]], axis=0)
            parts.append(big[:2 * srcs] + (big[2 * srcs:] + small * factor))
        trace[g, 0, :, here] = parts[0][:srcs] - parts[1][srcs:]
        trace[g, 1, :, here] = parts[1][:srcs] + parts[0][srcs:]

    def publish(g):
        @pl.when(has_right)
        def _():
            send_right(g).start()

        @pl.when(has_above)
        def _():
            send_up(g).start()

        out_ref[:, :, g * group_rows:(g + 1) * group_rows] = trace[g]

    @pl.when(first)
    def _():
        gather()

    for phase in range(2):
        @pl.when(True if phase == 0 else jnp.logical_not(first))
        def _():
            if phase == 1:
                gather()
            for g in range(groups):
                @pl.loop(0, blocks)
                def _(b):
                    if phase == 0:
                        convert(g * blocks + b)

                        @pl.when(first)
                        def _():
                            multiply(g, b)
                    else:
                        multiply(g, b)
                if phase == 0:
                    @pl.when(first)
                    def _():
                        publish(g)
                else:
                    publish(g)

    for g in range(groups):
        @pl.when(has_right)
        def _():
            send_right(g).wait_send()

        @pl.when(has_above)
        def _():
            send_up(g).wait_send()


def solution(mesh):
    ncol, nrow, nop = (mesh.shape[a] for a in ("sx", "sy", "op"))

    def shards(op_real, op_imag, coef_right, coef_upper, sources):
        rows, width = op_real.shape[2:]
        srcs = sources.shape[3]
        groups = rows // 256 if rows % 256 == 0 else rows // 128
        group_rows = rows // groups
        block = 256 if group_rows % 256 == 0 else 128
        vmem = pl.BlockSpec(memory_space=pltpu.VMEM)
        hbm = pl.BlockSpec(memory_space=pl.ANY)
        dma = pltpu.SemaphoreType.DMA
        out = pl.pallas_call(
            functools.partial(kernel, ncol, nrow, nop, groups, block),
            out_shape=jax.ShapeDtypeStruct((2, srcs, rows), F32),
            in_specs=[hbm, hbm, vmem, vmem, vmem],
            out_specs=vmem,
            scratch_shapes=[
                pltpu.VMEM((2, rows, width), BF16),
                pltpu.VMEM((2, rows, width), F8),
                pltpu.VMEM((SLOTS, 2, LOAD_ROWS, width), F32),
                pltpu.VMEM((nop, groups, 2, srcs, group_rows), F32),
                pltpu.VMEM((4 * srcs, width), BF16),
                pltpu.VMEM((2 * srcs, width), F8),
                pltpu.VMEM((srcs, 128), F32),
                pltpu.VMEM((groups, 2, srcs, group_rows), F32),
                pltpu.VMEM((groups, 2, srcs, group_rows), F32),
                pltpu.VMEM((groups, 2, srcs, group_rows), F32),
                dma((SLOTS, 2)),
                dma((groups, nop)),
                dma((groups, nop)),
                dma((groups,)),
                dma((groups,)),
                dma((groups,)),
                dma((groups,)),
            ],
            compiler_params=pltpu.CompilerParams(
                collective_id=0, has_side_effects=True, vmem_limit_bytes=67043328
            ),
        )(op_real[0, 0], op_imag[0, 0], coef_right[0, 0], coef_upper[0, 0], sources[0, 0])
        return out[None, None]

    return jax.shard_map(
        shards,
        mesh=mesh,
        in_specs=(
            P("sx", "sy", "op", None),
            P("sx", "sy", "op", None),
            P("sx", "sy", None, "op"),
            P("sx", "sy", None, "op"),
            P("sx", "sy", None, None, "op"),
        ),
        out_specs=P("sx", "sy", None, None, "op"),
        check_vma=False,
    )
```

profile of v0, /device:TPU:7, one launch (start us, length us, event | category | flops | bytes accessed | tf_op | source)
XLA Modules:
  0.0 161.0 jit_solution(9815297132062141750)
XLA Ops:
  0.0 159.4 %shard_map.55 = f32[2,16,1536]{2,1,0:T(8,128)} custom-call(f32[1536,6144]{1,0:T(8,128)} %bitcast.6, f32[1536,6144]{1,0:T(8,128)} %bitcast.7, f32[2,1536]{1,0:T(2,128)} %bitcast.10, f32[2,1536]{1,0:T(2,128)} %bitcast.11, f32[2,16,1536]{2,1,0:T(8,128)} %bitcast.9), custom_call_target="tpu_custom_call" | custom-call | tf_op jit(solution)/shard_map/pallas_call | solution.py:234
  159.4 1.6 %copy.7 = f32[1,1,2,16,1536]{4,3,2,1,0:T(8,128)} copy(f32[1,1,2,16,1536]{4,3,2,1,0:T(8,128)} %bitcast.8) | data formatting | bytes 393216
where the time goes:
time: 161 us
  Pallas kernels  159 us (99%)
  local copies, waits for them, and re-layouts  1.62 us (1%)
    pallas_call x1, Pallas kernels, shards(): pl.pallas_call(functools.partial(kernel, ncol, nrow, nop, groups, block),...  159 us

commit v1 on v0

--- a/solution.py
+++ b/solution.py
@@ -8,17 +8,16 @@
 from jax.sharding import PartitionSpec as P
 
 MESH = pl.DeviceIdType.MESH
-LOAD_ROWS = 32
-SLOTS = 3
+LANES = 128
 LOW_SCALE = 2.0**20
 F8 = jnp.float8_e4m3fn
 F32 = jnp.float32
 BF16 = jnp.bfloat16
-NT = (((1,), (1,)), ((), ()))
+NN = (((1,), (0,)), ((), ()))
 
 
 def kernel(
-    ncol, nrow, nop, groups, block,
+    ncol, nrow, nop, groups, pieces,
     real_hbm, imag_hbm, right_ref, upper_ref, src_ref, out_ref,
     high, low, stage, gathered, xw, x8, inv, left_buf, below_buf, trace,
     load_sem, gsend, grecv, lsend, lrecv, usend, urecv,
@@ -30,20 +29,21 @@
     rows, width = real_hbm.shape
     srcs = src_ref.shape[1]
     group_rows = rows // groups
-    chunks = rows // LOAD_ROWS
-    per_block = block // LOAD_ROWS
-    blocks = group_rows // block
+    split = group_rows // LANES
+    piece = width // pieces
+    blocks = rows // LANES
     ops = (real_hbm, imag_hbm)
 
-    def load(chunk, slot, k):
-        at = pl.multiple_of(chunk * LOAD_ROWS, LOAD_ROWS)
+    def load(blk, k, p):
+        slot = k * pieces + p
+        at = pl.multiple_of(blk * LANES, LANES)
         return pltpu.make_async_copy(
-            ops[k].at[pl.ds(at, LOAD_ROWS), :], stage.at[slot, k], load_sem.at[slot, k]
-        )
-
-    for s in range(SLOTS):
-        for k in range(2):
-            load(s, s, k).start()
+            ops[k].at[pl.ds(at, LANES), pl.ds(p * piece, piece)], stage.at[slot], load_sem.at[slot]
+        )
+
+    for k in range(2):
+        for p in range(pieces):
+            load(0, k, p).start()
 
     barrier = pltpu.get_barrier_semaphore()
     for j in range(1, nop):
@@ -124,52 +124,52 @@
         @pl.loop(0, nop * groups)
         def _(step):
             zz, g = step // groups, lax.rem(step, groups)
-            at = pl.multiple_of(step * group_rows, group_rows)
-            for k in range(2):
-                value = gathered[zz, g, k]
+            for h in range(split):
+                lanes = slice(h * LANES, (h + 1) * LANES)
+                at = step * split + h
+                for k in range(2):
+                    value = gathered[zz, g, k, :, lanes]
+                    top_part = value.astype(BF16)
+                    xw[at, k * srcs:(k + 1) * srcs, :] = top_part
+                    xw[at, (2 + k) * srcs:(3 + k) * srcs, :] = (
+                        value - top_part.astype(F32)
+                    ).astype(BF16)
+                both = jnp.concatenate(
+                    [gathered[zz, g, 0, :, lanes] * scale, gathered[zz, g, 1, :, lanes] * scale],
+                    axis=0,
+                )
+                x8[at] = both.astype(F8)
+
+    def convert(blk):
+        for k in range(2):
+            for p in range(pieces):
+                load(blk, k, p).wait()
+                value = stage[k * pieces + p].T
                 top_part = value.astype(BF16)
-                xw[k * srcs:(k + 1) * srcs, pl.ds(at, group_rows)] = top_part
-                xw[(2 + k) * srcs:(3 + k) * srcs, pl.ds(at, group_rows)] = (
-                    value - top_part.astype(F32)
-                ).astype(BF16)
-            both = jnp.concatenate([gathered[zz, g, 0] * scale, gathered[zz, g, 1] * scale], axis=0)
-            x8[:, pl.ds(at, group_rows)] = both.astype(F8)
-
-    def convert(b):
-        @pl.loop(0, per_block)
-        def _(i):
-            chunk = b * per_block + i
-            slot = lax.rem(chunk, SLOTS)
-            at = pl.multiple_of(chunk * LOAD_ROWS, LOAD_ROWS)
-            for k in range(2):
-                load(chunk, slot, k).wait()
-
-                @pl.loop(0, width // 512)
-                def _(q):
-                    cols = pl.ds(pl.multiple_of(q * 512, 512), 512)
-                    value = stage[slot, k, :, cols]
-                    top_part = value.astype(BF16)
-                    high[k, pl.ds(at, LOAD_ROWS), cols] = top_part
-                    low[k, pl.ds(at, LOAD_ROWS), cols] = (
-                        (value - top_part.astype(F32)) * LOW_SCALE
-                    ).astype(F8)
-
-            @pl.when(chunk + SLOTS < chunks)
-            def _():
-                for k in range(2):
-                    load(chunk + SLOTS, slot, k).start()
-
-    def multiply(g, b):
-        at = pl.ds(pl.multiple_of((g * blocks + b) * block, block), block)
-        here = pl.ds(pl.multiple_of(b * block, block), block)
+                cols = slice(p * piece, (p + 1) * piece)
+                high[k, blk, cols, :] = top_part
+                low[k, blk, cols, :] = ((value - top_part.astype(F32)) * LOW_SCALE).astype(F8)
+
+                @pl.when(blk + 1 < blocks)
+                def _():
+                    load(blk + 1, k, p).start()
+
+    def side(ref):
+        return jnp.concatenate([ref[j] for j in range(width // LANES)], axis=1)
+
+    def weights(ref, k, g):
+        return jnp.concatenate([ref[k, g * split + h] for h in range(split)], axis=1)
+
+    def multiply(g):
         parts = []
+        wide, narrow = side(xw), side(x8)
+        factor = jnp.concatenate([inv[:, :1], inv[:, :1]], axis=0)
         for k in range(2):
-            big = lax.dot_general(high[k, at, :], xw[...], NT, preferred_element_type=F32).T
-            small = lax.dot_general(low[k, at, :], x8[...], NT, preferred_element_type=F32).T
-            factor = jnp.concatenate([inv[:, :1], inv[:, :1]], axis=0)
+            big = lax.dot_general(wide, weights(high, k, g), NN, preferred_element_type=F32)
+            small = lax.dot_general(narrow, weights(low, k, g), NN, preferred_element_type=F32)
             parts.append(big[:2 * srcs] + (big[2 * srcs:] + small * factor))
-        trace[g, 0, :, here] = parts[0][:srcs] - parts[1][srcs:]
-        trace[g, 1, :, here] = parts[1][:srcs] + parts[0][srcs:]
+        trace[g, 0] = parts[0][:srcs] - parts[1][srcs:]
+        trace[g, 1] = parts[1][:srcs] + parts[0][srcs:]
 
     def publish(g):
         @pl.when(has_right)
@@ -180,34 +180,31 @@
         def _():
             send_up(g).start()
 
-        out_ref[:, :, g * group_rows:(g + 1) * group_rows] = trace[g]
+        out_ref[:, :, pl.ds(pl.multiple_of(g * group_rows, LANES), group_rows)] = trace[g]
 
     @pl.when(first)
     def _():
         gather()
 
-    for phase in range(2):
-        @pl.when(True if phase == 0 else jnp.logical_not(first))
-        def _():
-            if phase == 1:
-                gather()
-            for g in range(groups):
-                @pl.loop(0, blocks)
-                def _(b):
-                    if phase == 0:
-                        convert(g * blocks + b)
-
-                        @pl.when(first)
-                        def _():
-                            multiply(g, b)
-                    else:
-                        multiply(g, b)
-                if phase == 0:
-                    @pl.when(first)
-                    def _():
-                        publish(g)
-                else:
-                    publish(g)
+    @pl.loop(0, groups)
+    def _(g):
+        @pl.loop(0, split)
+        def _(h):
+            convert(g * split + h)
+
+        @pl.when(first)
+        def _():
+            multiply(g)
+            publish(g)
+
+    @pl.when(jnp.logical_not(first))
+    def _():
+        gather()
+
+        @pl.loop(0, groups)
+        def _(g):
+            multiply(g)
+            publish(g)
 
     for g in range(groups):
         @pl.when(has_right)
@@ -227,27 +224,27 @@
         srcs = sources.shape[3]
         groups = rows // 256 if rows % 256 == 0 else rows // 128
         group_rows = rows // groups
-        block = 256 if group_rows % 256 == 0 else 128
+        pieces = 2 if width % 256 == 0 else 1
         vmem = pl.BlockSpec(memory_space=pltpu.VMEM)
         hbm = pl.BlockSpec(memory_space=pl.ANY)
         dma = pltpu.SemaphoreType.DMA
         out = pl.pallas_call(
-            functools.partial(kernel, ncol, nrow, nop, groups, block),
+            functools.partial(kernel, ncol, nrow, nop, groups, pieces),
             out_shape=jax.ShapeDtypeStruct((2, srcs, rows), F32),
             in_specs=[hbm, hbm, vmem, vmem, vmem],
             out_specs=vmem,
             scratch_shapes=[
-                pltpu.VMEM((2, rows, width), BF16),
-                pltpu.VMEM((2, rows, width), F8),
-                pltpu.VMEM((SLOTS, 2, LOAD_ROWS, width), F32),
+                pltpu.VMEM((2, rows // LANES, width, LANES), BF16),
+                pltpu.VMEM((2, rows // LANES, width, LANES), F8),
+                pltpu.VMEM((2 * pieces, LANES, width // pieces), F32),
                 pltpu.VMEM((nop, groups, 2, srcs, group_rows), F32),
-                pltpu.VMEM((4 * srcs, width), BF16),
-                pltpu.VMEM((2 * srcs, width), F8),
+                pltpu.VMEM((width // LANES, 4 * srcs, LANES), BF16),
+                pltpu.VMEM((width // LANES, 2 * srcs, LANES), F8),
                 pltpu.VMEM((srcs, 128), F32),
                 pltpu.VMEM((groups, 2, srcs, group_rows), F32),
                 pltpu.VMEM((groups, 2, srcs, group_rows), F32),
                 pltpu.VMEM((groups, 2, srcs, group_rows), F32),
-                dma((SLOTS, 2)),
+                dma((2 * pieces,)),
                 dma((groups, nop)),
                 dma((groups, nop)),
                 dma((groups,)),

time: 161 us -> 126 us (0.78)
  Pallas kernels: 159 us -> 124 us
    pallas_call x1, Pallas kernels: 159 us -> 124 us  [shards(): pl.pallas_call(functools.partial(kernel, ncol, nrow, nop, groups, pieces)...]
where the time goes in v1:
time: 126 us
  Pallas kernels  124 us (98%)
  local copies, waits for them, and re-layouts  1.62 us (1%)
    pallas_call x1, Pallas kernels, shards(): pl.pallas_call(functools.partial(kernel, ncol, nrow, nop, groups, pieces)...  124 us

profile of v1, /device:TPU:7, one launch (start us, length us, event | category | flops | bytes accessed | tf_op | source)
XLA Modules:
  0.0 126.1 jit_solution(394559479400164618)
XLA Ops:
  0.0 124.5 %shard_map.55 = f32[2,16,1536]{2,1,0:T(8,128)} custom-call(f32[1536,6144]{1,0:T(8,128)} %bitcast.6, f32[1536,6144]{1,0:T(8,128)} %bitcast.7, f32[2,1536]{1,0:T(2,128)} %bitcast.10, f32[2,1536]{1,0:T(2,128)} %bitcast.11, f32[2,16,1536]{2,1,0:T(8,128)} %bitcast.9), custom_call_target="tpu_custom_call" | custom-call | tf_op jit(solution)/shard_map/pallas_call | solution.py:231
  124.5 1.6 %copy.7 = f32[1,1,2,16,1536]{4,3,2,1,0:T(8,128)} copy(f32[1,1,2,16,1536]{4,3,2,1,0:T(8,128)} %bitcast.8) | data formatting | bytes 393216

commit v2 on v1

v2 whole, which is shorter than its diff:
```python
import functools

import jax
import jax.numpy as jnp
from jax import lax
from jax.experimental import pallas as pl
from jax.experimental.pallas import tpu as pltpu
from jax.sharding import PartitionSpec as P

MESH = pl.DeviceIdType.MESH
LANES = 128
STREAM_SLOTS = 6
AHEAD = 2
PIECES = 3
LOAD_SLOTS = 5
LOW_SCALE = 2.0**20
F8 = jnp.float8_e4m3fn
F32 = jnp.float32
BF16 = jnp.bfloat16
NN = (((1,), (0,)), ((), ()))
NT = (((1,), (1,)), ((), ()))


def kernel(
    ncol, nrow, nop, groups, pieces,
    real_hbm, imag_hbm, right_ref, upper_ref, src_ref, out_ref,
    gathered, xw, x8, inv, left_buf, below_buf, trace,
    load_sem, gsend, grecv, lsend, lrecv, usend, urecv,
):
    c = lax.axis_index("sx")
    r = lax.axis_index("sy")
    z = lax.axis_index("op")
    first = c + r == 0
    rows, width = real_hbm.shape
    srcs = src_ref.shape[1]
    group_rows = rows // groups
    split = group_rows // LANES
    piece = width // pieces
    blocks = rows // LANES
    ops = (real_hbm, imag_hbm)
    has_left, has_right = c > 0, c < ncol - 1
    has_below, has_above = r > 0, r < nrow - 1

    def meet():
        barrier = pltpu.get_barrier_semaphore()
        for j in range(1, nop):
            pl.semaphore_signal(
                barrier, inc=1, device_id=(c, r, lax.rem(z + j, nop)), device_id_type=MESH
            )

        def greet(cond, cc, rr):
            @pl.when(cond)
            def _():
                pl.semaphore_signal(barrier, inc=1, device_id=(cc, rr, z), device_id_type=MESH)

        greet(has_left, c - 1, r)
        greet(has_right, c + 1, r)
        greet(has_below, c, r - 1)
        greet(has_above, c, r + 1)
        near = sum(jnp.where(cond, 1, 0) for cond in (has_left, has_right, has_below, has_above))
        pl.semaphore_wait(barrier, nop - 1 + near)

    def send_right(g):
        return pltpu.make_async_remote_copy(
            trace.at[g], left_buf.at[g], lsend.at[g], lrecv.at[g],
            device_id=(c + 1, r, z), device_id_type=MESH,
        )

    def send_up(g):
        return pltpu.make_async_remote_copy(
            trace.at[g], below_buf.at[g], usend.at[g], urecv.at[g],
            device_id=(c, r + 1, z), device_id_type=MESH,
        )

    def share(g, j):
        peer = lax.rem(z + j, nop)
        return pltpu.make_async_remote_copy(
            gathered.at[z, g], gathered.at[z, g], gsend.at[g, j], grecv.at[g, j],
            device_id=(c, r, peer), device_id_type=MESH,
        )

    def span(g):
        return pl.ds(pl.multiple_of(g * group_rows, LANES), group_rows)

    def publish(g):
        @pl.when(has_right)
        def _():
            send_right(g).start()

        @pl.when(has_above)
        def _():
            send_up(g).start()

        out_ref[:, :, span(g)] = trace[g]

    def arrive(g):
        cols = span(g)
        gathered[z, g] = src_ref[:, :, cols]

        def add(coef_ref, buf):
            cr = coef_ref[0:1, cols]
            ci = coef_ref[1:2, cols]
            gathered[z, g, 0] += cr * buf[g, 0] - ci * buf[g, 1]
            gathered[z, g, 1] += cr * buf[g, 1] + ci * buf[g, 0]

        @pl.when(has_left)
        def _():
            send_right(g).wait_recv()
            add(right_ref, left_buf)

        @pl.when(has_below)
        def _():
            send_up(g).wait_recv()
            add(upper_ref, below_buf)

        for j in range(1, nop):
            share(g, j).start()

    def prepare(steps, slot):
        most = None
        for zz, g in steps:
            both = jnp.maximum(jnp.abs(gathered[zz, g, 0]), jnp.abs(gathered[zz, g, 1]))
            most = both if most is None else jnp.maximum(most, both)
        top = jnp.maximum(jnp.max(most, axis=1, keepdims=True), 1e-30)
        scale = 256.0 / top
        back = top * (1.0 / (256.0 * LOW_SCALE))
        inv[slot] = jnp.broadcast_to(jnp.concatenate([back, back], axis=0), (2 * srcs, LANES))
        for zz, g in steps:
            for h in range(split):
                lanes = slice(h * LANES, (h + 1) * LANES)
                at = (zz * groups + g) * split + h
                for k in range(2):
                    value = gathered[zz, g, k, :, lanes]
                    top_part = value.astype(BF16)
                    xw[at, k * srcs:(k + 1) * srcs, :] = top_part
                    xw[at, (2 + k) * srcs:(3 + k) * srcs, :] = (
                        value - top_part.astype(F32)
                    ).astype(BF16)
                x8[at] = jnp.concatenate(
                    [gathered[zz, g, 0, :, lanes] * scale, gathered[zz, g, 1, :, lanes] * scale],
                    axis=0,
                ).astype(F8)

    def side(ref, steps):
        return jnp.concatenate(
            [ref[(zz * groups + g) * split + h] for zz, g in steps for h in range(split)], axis=1
        )

    def merge(big, small, slot):
        return big[:2 * srcs] + (big[2 * srcs:] + small * inv[slot][:, :1])

    def stream(stage):
        slots = stage.shape[0]
        seg = rows
        paired = (groups - 1) // 2 * 2
        early = nop * paired
        half = nop // 2
        chunks = early + 2 * half * (groups - paired)

        def units(i):
            k = lax.rem(i, 2)
            a, b = i // 2, (i - early) // 2
            in_pairs = i < early
            first_m = jnp.where(in_pairs, 2 * lax.rem(a, paired // 2), paired + b // half)
            first_j = jnp.where(in_pairs, a // (paired // 2), 2 * lax.rem(b, half))
            second_m = jnp.where(in_pairs, first_m + 1, first_m)
            second_j = jnp.where(in_pairs, first_j, first_j + 1)
            return k, ((first_m, first_j), (second_m, second_j))

        def owner(j):
            return lax.rem(z - j + nop, nop)

        def load(i, u, op_k):
            _, pair = units(i)
            m, j = pair[u]
            slot = lax.rem(i, slots)
            return pltpu.make_async_copy(
                ops[op_k].at[
                    pl.ds(pl.multiple_of(m * group_rows, LANES), group_rows),
                    pl.ds(pl.multiple_of(owner(j) * seg, LANES), seg),
                ],
                stage.at[slot, u], load_sem.at[slot, u],
            )

        def fetch(i, op_k):
            for u in range(2):
                load(i, u, op_k).start()

        for i in range(slots):
            fetch(i, i % 2)
        meet()
        for g in range(groups):
            gathered[z, g] = src_ref[:, :, g * group_rows:(g + 1) * group_rows]
        for g in range(groups):
            for j in range(1, nop):
                share(g, j).start()
        trace[...] = jnp.zeros_like(trace)

        def chunk(i, op_k):
            _, pair = units(i)
            slot = lax.rem(i, slots)
            for u in range(2):
                load(i, u, op_k).wait()
            for u in range(2):
                m, j = pair[u]
                steps = [(owner(j), g) for g in range(groups)]
                value = stage[slot, u]
                top_part = value.astype(BF16)
                rest = ((value - top_part.astype(F32)) * LOW_SCALE).astype(F8)
                big = lax.dot_general(side(xw, steps), top_part, NT, preferred_element_type=F32)
                small = lax.dot_general(side(x8, steps), rest, NT, preferred_element_type=F32)
                part = merge(big, small, j)
                if op_k == 0:
                    trace[m, 0] += part[:srcs]
                    trace[m, 1] += part[srcs:]
                else:
                    trace[m, 0] -= part[srcs:]
                    trace[m, 1] += part[:srcs]

            @pl.when(i + slots < chunks)
            def _():
                fetch(i + slots, op_k)

        @pl.loop(0, nop)
        def _(j):
            @pl.when(j > 0)
            def _():
                for g in range(groups):
                    share(g, j).wait()

            prepare([(owner(j), g) for g in range(groups)], j)

            @pl.loop(0, paired // 2)
            def _(a):
                for op_k in range(2):
                    chunk(2 * (j * (paired // 2) + a) + op_k, op_k)

        @pl.loop(0, paired)
        def _(m):
            publish(m)

        @pl.loop(0, groups - paired)
        def _(n):
            @pl.loop(0, half)
            def _(b):
                for op_k in range(2):
                    chunk(early + 2 * (n * half + b) + op_k, op_k)

            publish(paired + n)

    def resident(stage, high, low):
        slots = stage.shape[0]
        per = 2 * pieces
        chunks = per * blocks

        def load(i, n):
            k, p = n // pieces, n % pieces
            at = pl.multiple_of((i // per) * LANES, LANES)
            slot = lax.rem(i, slots)
            return pltpu.make_async_copy(
                ops[k].at[pl.ds(at, LANES), pl.ds(p * piece, piece)],
                stage.at[slot], load_sem.at[slot, 0],
            )

        for i in range(slots):
            load(i, i % per).start()
        meet()

        @pl.loop(0, blocks)
        def _(blk):
            for n in range(per):
                i = blk * per + n
                load(i, n).wait()
                value = stage[lax.rem(i, slots)].T
                top_part = value.astype(BF16)
                k, p = n // pieces, n % pieces
                cols = slice(p * piece, (p + 1) * piece)
                high[k, blk, cols, :] = top_part
                low[k, blk, cols, :] = ((value - top_part.astype(F32)) * LOW_SCALE).astype(F8)

                @pl.when(i + slots < chunks)
                def _():
                    load(i + slots, (n + slots) % per).start()

        trace[...] = jnp.zeros_like(trace)

        def weights(ref, k, m, g):
            tiles = []
            for zz in range(nop):
                at = pl.ds(pl.multiple_of(zz * rows + g * group_rows, LANES), group_rows)
                tiles.append(jnp.concatenate(
                    [ref[k, m * split + h, at, :] for h in range(split)], axis=1
                ))
            return jnp.concatenate(tiles, axis=0)

        def multiply(m, g):
            steps = [(zz, g) for zz in range(nop)]
            wide, narrow = side(xw, steps), side(x8, steps)
            parts = []
            for k in range(2):
                big = lax.dot_general(wide, weights(high, k, m, g), NN, preferred_element_type=F32)
                small = lax.dot_general(narrow, weights(low, k, m, g), NN, preferred_element_type=F32)
                parts.append(merge(big, small, g))
            trace[m, 0] += parts[0][:srcs] - parts[1][srcs:]
            trace[m, 1] += parts[1][:srcs] + parts[0][srcs:]

        together = 2 if groups % 2 == 0 else 1
        for g in range(min(AHEAD, groups)):
            arrive(g)

        @pl.loop(0, groups)
        def _(g):
            @pl.when(g + AHEAD < groups)
            def _():
                arrive(g + AHEAD)

            for j in range(1, nop):
                share(g, j).wait()
            prepare([(zz, g) for zz in range(nop)], g)

            @pl.loop(0, groups // together)
            def _(a):
                for n in range(together):
                    multiply(a * together + n, g)

                @pl.when(g == groups - 1)
                def _():
                    for n in range(together):
                        publish(a * together + n)

    @pl.when(first)
    def _():
        pl.run_scoped(stream, pltpu.VMEM((STREAM_SLOTS, 2, group_rows, rows), F32))

    @pl.when(jnp.logical_not(first))
    def _():
        pl.run_scoped(
            resident,
            pltpu.VMEM((LOAD_SLOTS, LANES, piece), F32),
            pltpu.VMEM((2, blocks, width, LANES), BF16),
            pltpu.VMEM((2, blocks, width, LANES), F8),
        )

    for g in range(groups):
        @pl.when(has_right)
        def _():
            send_right(g).wait_send()

        @pl.when(has_above)
        def _():
            send_up(g).wait_send()


def solution(mesh):
    ncol, nrow, nop = (mesh.shape[a] for a in ("sx", "sy", "op"))

    def shards(op_real, op_imag, coef_right, coef_upper, sources):
        rows, width = op_real.shape[2:]
        srcs = sources.shape[3]
        groups = rows // 256 if rows % 256 == 0 else rows // 128
        group_rows = rows // groups
        pieces = PIECES if width % (PIECES * LANES) == 0 else 1
        vmem = pl.BlockSpec(memory_space=pltpu.VMEM)
        hbm = pl.BlockSpec(memory_space=pl.ANY)
        dma = pltpu.SemaphoreType.DMA
        out = pl.pallas_call(
            functools.partial(kernel, ncol, nrow, nop, groups, pieces),
            out_shape=jax.ShapeDtypeStruct((2, srcs, rows), F32),
            in_specs=[hbm, hbm, vmem, vmem, vmem],
            out_specs=vmem,
            scratch_shapes=[
                pltpu.VMEM((nop, groups, 2, srcs, group_rows), F32),
                pltpu.VMEM((width // LANES, 4 * srcs, LANES), BF16),
                pltpu.VMEM((width // LANES, 2 * srcs, LANES), F8),
                pltpu.VMEM((max(groups, nop), 2 * srcs, LANES), F32),
                pltpu.VMEM((groups, 2, srcs, group_rows), F32),
                pltpu.VMEM((groups, 2, srcs, group_rows), F32),
                pltpu.VMEM((groups, 2, srcs, group_rows), F32),
                dma((max(STREAM_SLOTS, LOAD_SLOTS), 2)),
                dma((groups, nop)),
                dma((groups, nop)),
                dma((groups,)),
                dma((groups,)),
                dma((groups,)),
                dma((groups,)),
            ],
            compiler_params=pltpu.CompilerParams(
                collective_id=0, has_side_effects=True, vmem_limit_bytes=67043328
            ),
        )(op_real[0, 0], op_imag[0, 0], coef_right[0, 0], coef_upper[0, 0], sources[0, 0])
        return out[None, None]

    return jax.shard_map(
        shards,
        mesh=mesh,
        in_specs=(
            P("sx", "sy", "op", None),
            P("sx", "sy", "op", None),
            P("sx", "sy", None, "op"),
            P("sx", "sy", None, "op"),
            P("sx", "sy", None, None, "op"),
        ),
        out_specs=P("sx", "sy", None, None, "op"),
        check_vma=False,
    )
```

time: 126 us -> 102 us (0.81)
  Pallas kernels: 124 us -> 101 us
    pallas_call x1, Pallas kernels: 124 us -> 101 us  [shards(): pl.pallas_call(functools.partial(kernel, ncol, nrow, nop, groups, pieces)...]
where the time goes in v2:
time: 102 us
  Pallas kernels  101 us (99%)
  local copies, waits for them, and re-layouts  1.62 us (2%)
    pallas_call x1, Pallas kernels, shards(): pl.pallas_call(functools.partial(kernel, ncol, nrow, nop, groups, pieces)...  101 us

profile of v2, /device:TPU:7, one launch (start us, length us, event | category | flops | bytes accessed | tf_op | source)
XLA Modules:
  0.0 102.2 jit_solution(14534091358892937305)
XLA Ops:
  0.0 100.6 %shard_map.55 = f32[2,16,1536]{2,1,0:T(8,128)} custom-call(f32[1536,6144]{1,0:T(8,128)} %bitcast.6, f32[1536,6144]{1,0:T(8,128)} %bitcast.7, f32[2,1536]{1,0:T(2,128)} %bitcast.10, f32[2,1536]{1,0:T(2,128)} %bitcast.11, f32[2,16,1536]{2,1,0:T(8,128)} %bitcast.9), custom_call_target="tpu_custom_call" | custom-call | tf_op jit(solution)/shard_map/pallas_call | solution.py:366
  100.6 1.6 %copy.7 = f32[1,1,2,16,1536]{4,3,2,1,0:T(8,128)} copy(f32[1,1,2,16,1536]{4,3,2,1,0:T(8,128)} %bitcast.8) | data formatting | bytes 393216

commit v3 on v2

--- a/solution.py
+++ b/solution.py
@@ -24,8 +24,8 @@
 def kernel(
     ncol, nrow, nop, groups, pieces,
     real_hbm, imag_hbm, right_ref, upper_ref, src_ref, out_ref,
-    gathered, xw, x8, inv, left_buf, below_buf, trace,
-    load_sem, gsend, grecv, lsend, lrecv, usend, urecv,
+    gathered, xw, x8, inv, mix, trace, mate_right, mate_upper, mate_src,
+    load_sem, hsend, msend, grecv, lsend, lrecv, psend, precv,
 ):
     c = lax.axis_index("sx")
     r = lax.axis_index("sy")
@@ -41,80 +41,114 @@
     has_left, has_right = c > 0, c < ncol - 1
     has_below, has_above = r > 0, r < nrow - 1
 
+    mate = 1 - r
+    order = [nop // 2] if nop % 2 == 0 else []
+    for j in range((nop - 1) // 2, 0, -1):
+        order = [j, nop - j] + order
+
+    def swap():
+        pairs = ((right_ref, mate_right), (upper_ref, mate_upper), (src_ref, mate_src))
+        return [
+            pltpu.make_async_remote_copy(
+                mine, theirs, psend.at[n], precv.at[n],
+                device_id=(c, mate, z), device_id_type=MESH,
+            )
+            for n, (mine, theirs) in enumerate(pairs)
+        ]
+
     def meet():
         barrier = pltpu.get_barrier_semaphore()
+
+        def greet(cc, rr, zz):
+            pl.semaphore_signal(barrier, inc=1, device_id=(cc, rr, zz), device_id_type=MESH)
+
+        greet(c, mate, z)
         for j in range(1, nop):
-            pl.semaphore_signal(
-                barrier, inc=1, device_id=(c, r, lax.rem(z + j, nop)), device_id_type=MESH
-            )
-
-        def greet(cond, cc, rr):
-            @pl.when(cond)
-            def _():
-                pl.semaphore_signal(barrier, inc=1, device_id=(cc, rr, z), device_id_type=MESH)
-
-        greet(has_left, c - 1, r)
-        greet(has_right, c + 1, r)
-        greet(has_below, c, r - 1)
-        greet(has_above, c, r + 1)
-        near = sum(jnp.where(cond, 1, 0) for cond in (has_left, has_right, has_below, has_above))
-        pl.semaphore_wait(barrier, nop - 1 + near)
+            peer = lax.rem(z + j, nop)
+            greet(c, r, peer)
+            greet(c, mate, peer)
+
+        @pl.when(has_left)
+        def _():
+            greet(c - 1, mate, z)
+
+        @pl.when(has_right)
+        def _():
+            greet(c + 1, mate, z)
+
+        near = jnp.where(has_left, 1, 0) + jnp.where(has_right, 1, 0)
+        pl.semaphore_wait(barrier, 2 * nop - 1 + near)
+        for copy in swap():
+            copy.start()
 
     def send_right(g):
         return pltpu.make_async_remote_copy(
-            trace.at[g], left_buf.at[g], lsend.at[g], lrecv.at[g],
-            device_id=(c + 1, r, z), device_id_type=MESH,
+            trace.at[g], mix.at[g], lsend.at[g], lrecv.at[g],
+            device_id=(c + 1, mate, z), device_id_type=MESH,
         )
 
-    def send_up(g):
+    def lent(g, j):
         return pltpu.make_async_remote_copy(
-            trace.at[g], below_buf.at[g], usend.at[g], urecv.at[g],
-            device_id=(c, r + 1, z), device_id_type=MESH,
+            mix.at[g], gathered.at[z, g], hsend.at[g, j], grecv.at[g, j],
+            device_id=(c, mate, lax.rem(z + j, nop)), device_id_type=MESH,
         )
 
-    def share(g, j):
-        peer = lax.rem(z + j, nop)
+    def passed(g, j):
         return pltpu.make_async_remote_copy(
-            gathered.at[z, g], gathered.at[z, g], gsend.at[g, j], grecv.at[g, j],
-            device_id=(c, r, peer), device_id_type=MESH,
+            gathered.at[z, g], gathered.at[z, g], msend.at[g, j], grecv.at[g, j],
+            device_id=(c, r, lax.rem(z + j, nop)), device_id_type=MESH,
         )
+
+    def each(g, j, by_mate, act):
+        if 2 * j == nop:
+            @pl.when(lax.rem(g, 2) == (0 if by_mate else 1))
+            def _():
+                act(g, j)
+        elif (2 * j < nop) == by_mate:
+            act(g, j)
+
+    def start_lent(g, j):
+        lent(g, j).start()
+
+    def start_passed(g, j):
+        passed(g, j).start()
 
     def span(g):
         return pl.ds(pl.multiple_of(g * group_rows, LANES), group_rows)
 
+    def combine(g, with_left, with_own):
+        cols = span(g)
+
+        def term(coef_ref, buf, k):
+            cr = coef_ref[0:1, cols]
+            ci = coef_ref[1:2, cols]
+            if k == 0:
+                return cr * buf[g, 0] - ci * buf[g, 1]
+            return cr * buf[g, 1] + ci * buf[g, 0]
+
+        values = [mate_src[k, :, cols] for k in range(2)]
+        if with_left:
+            send_right(g).wait_recv()
+            values = [values[k] + term(mate_right, mix, k) for k in range(2)]
+        if with_own:
+            values = [values[k] + term(mate_upper, trace, k) for k in range(2)]
+        for k in range(2):
+            mix[g, k] = values[k]
+        lent(g, 0).start()
+        for j in order:
+            each(g, j, True, start_lent)
+
     def publish(g):
         @pl.when(has_right)
         def _():
             send_right(g).start()
 
-        @pl.when(has_above)
-        def _():
-            send_up(g).start()
-
         out_ref[:, :, span(g)] = trace[g]
 
-    def arrive(g):
-        cols = span(g)
-        gathered[z, g] = src_ref[:, :, cols]
-
-        def add(coef_ref, buf):
-            cr = coef_ref[0:1, cols]
-            ci = coef_ref[1:2, cols]
-            gathered[z, g, 0] += cr * buf[g, 0] - ci * buf[g, 1]
-            gathered[z, g, 1] += cr * buf[g, 1] + ci * buf[g, 0]
-
-        @pl.when(has_left)
-        def _():
-            send_right(g).wait_recv()
-            add(right_ref, left_buf)
-
-        @pl.when(has_below)
-        def _():
-            send_up(g).wait_recv()
-            add(upper_ref, below_buf)
-
-        for j in range(1, nop):
-            share(g, j).start()
+    def take(g):
+        passed(g, 0).wait_recv()
+        for j in order:
+            each(g, j, False, start_passed)
 
     def prepare(steps, slot):
         most = None
@@ -167,8 +201,11 @@
             second_j = jnp.where(in_pairs, first_j, first_j + 1)
             return k, ((first_m, first_j), (second_m, second_j))
 
-        def owner(j):
-            return lax.rem(z - j + nop, nop)
+        def hop(n):
+            return jnp.where(lax.rem(n, 2) == 1, (n + 1) // 2, lax.rem(nop - n // 2, nop))
+
+        def owner(n):
+            return lax.rem(z - hop(n) + nop, nop)
 
         def load(i, u, op_k):
             _, pair = units(i)
@@ -191,9 +228,9 @@
         meet()
         for g in range(groups):
             gathered[z, g] = src_ref[:, :, g * group_rows:(g + 1) * group_rows]
-        for g in range(groups):
-            for j in range(1, nop):
-                share(g, j).start()
+        for j in order:
+            for g in range(groups):
+                each(g, j, False, start_passed)
         trace[...] = jnp.zeros_like(trace)
 
         def chunk(i, op_k):
@@ -226,7 +263,7 @@
             @pl.when(j > 0)
             def _():
                 for g in range(groups):
-                    share(g, j).wait()
+                    passed(g, hop(j)).wait_recv()
 
             prepare([(owner(j), g) for g in range(groups)], j)
 
@@ -235,9 +272,16 @@
                 for op_k in range(2):
                     chunk(2 * (j * (paired // 2) + a) + op_k, op_k)
 
+        for copy in swap():
+            copy.wait_recv()
+
+        def give(m):
+            publish(m)
+            combine(m, False, True)
+
         @pl.loop(0, paired)
         def _(m):
-            publish(m)
+            give(m)
 
         @pl.loop(0, groups - paired)
         def _(n):
@@ -246,7 +290,7 @@
                 for op_k in range(2):
                     chunk(early + 2 * (n * half + b) + op_k, op_k)
 
-            publish(paired + n)
+            give(paired + n)
 
     def resident(stage, high, low):
         slots = stage.shape[0]
@@ -265,6 +309,16 @@
         for i in range(slots):
             load(i, i % per).start()
         meet()
+        for copy in swap():
+            copy.wait_recv()
+
+        @pl.when(c == 0)
+        def _():
+            for g in range(groups):
+                mix[g] = mate_src[:, :, g * group_rows:(g + 1) * group_rows]
+            for j in order:
+                for g in range(groups):
+                    each(g, j, True, start_lent)
 
         @pl.loop(0, blocks)
         def _(blk):
@@ -304,18 +358,27 @@
             trace[m, 0] += parts[0][:srcs] - parts[1][srcs:]
             trace[m, 1] += parts[1][:srcs] + parts[0][srcs:]
 
-        together = 2 if groups % 2 == 0 else 1
-        for g in range(min(AHEAD, groups)):
-            arrive(g)
+        @pl.when(jnp.logical_and(r == 1, c > 0))
+        def _():
+            @pl.loop(0, groups)
+            def _(g):
+                combine(g, True, False)
+
+        together = 3 if groups % 3 == 0 else 1
+        ahead = jnp.where(c + r == 1, 1, AHEAD)
+
+        @pl.loop(0, ahead)
+        def _(g):
+            take(g)
 
         @pl.loop(0, groups)
         def _(g):
-            @pl.when(g + AHEAD < groups)
+            @pl.when(g + ahead < groups)
             def _():
-                arrive(g + AHEAD)
+                take(g + ahead)
 
             for j in range(1, nop):
-                share(g, j).wait()
+                passed(g, j).wait_recv()
             prepare([(zz, g) for zz in range(nop)], g)
 
             @pl.loop(0, groups // together)
@@ -327,6 +390,12 @@
                 def _():
                     for n in range(together):
                         publish(a * together + n)
+
+        @pl.when(r == 0)
+        def _():
+            @pl.loop(0, groups)
+            def _(g):
+                combine(g, True, True)
 
     @pl.when(first)
     def _():
@@ -341,14 +410,28 @@
             pltpu.VMEM((2, blocks, width, LANES), F8),
         )
 
-    for g in range(groups):
+    for copy in swap():
+        copy.wait_send()
+
+    def sent_lent(g, j):
+        lent(g, j).wait_send()
+
+    def sent_passed(g, j):
+        passed(g, j).wait_send()
+
+    @pl.loop(0, groups)
+    def _(g):
         @pl.when(has_right)
         def _():
             send_right(g).wait_send()
 
-        @pl.when(has_above)
-        def _():
-            send_up(g).wait_send()
+        @pl.when(c + mate > 0)
+        def _():
+            lent(g, 0).wait_send()
+
+        for j in order:
+            each(g, j, True, sent_lent)
+            each(g, j, False, sent_passed)
 
 
 def solution(mesh):
@@ -375,14 +458,17 @@
                 pltpu.VMEM((max(groups, nop), 2 * srcs, LANES), F32),
                 pltpu.VMEM((groups, 2, srcs, group_rows), F32),
                 pltpu.VMEM((groups, 2, srcs, group_rows), F32),
-                pltpu.VMEM((groups, 2, srcs, group_rows), F32),
+                pltpu.VMEM((2, rows), F32),
+                pltpu.VMEM((2, rows), F32),
+                pltpu.VMEM((2, srcs, rows), F32),
                 dma((max(STREAM_SLOTS, LOAD_SLOTS), 2)),
+                dma((groups, nop)),
                 dma((groups, nop)),
                 dma((groups, nop)),
                 dma((groups,)),
                 dma((groups,)),
-                dma((groups,)),
-                dma((groups,)),
+                dma((3,)),
+                dma((3,)),
             ],
             compiler_params=pltpu.CompilerParams(
                 collective_id=0, has_side_effects=True, vmem_limit_bytes=67043328

time: 102 us -> 111 us (1.088)
  Pallas kernels: 101 us -> 110 us
    pallas_call x1, Pallas kernels: 101 us -> 110 us  [shards(): pl.pallas_call(functools.partial(kernel, ncol, nrow, nop, groups, pieces)...]
where the time goes in v3:
time: 111 us
  Pallas kernels  110 us (99%)
  local copies, waits for them, and re-layouts  1.62 us (1%)
    pallas_call x1, Pallas kernels, shards(): pl.pallas_call(functools.partial(kernel, ncol, nrow, nop, groups, pieces)...  110 us

profile of v3, /device:TPU:7, one launch (start us, length us, event | category | flops | bytes accessed | tf_op | source)
XLA Modules:
  0.0 111.3 jit_solution(13274788567737730260)
XLA Ops:
  0.0 109.7 %shard_map.55 = f32[2,16,1536]{2,1,0:T(8,128)} custom-call(f32[1536,6144]{1,0:T(8,128)} %bitcast.6, f32[1536,6144]{1,0:T(8,128)} %bitcast.7, f32[2,1536]{1,0:T(2,128)} %bitcast.10, f32[2,1536]{1,0:T(2,128)} %bitcast.11, f32[2,16,1536]{2,1,0:T(8,128)} %bitcast.9), custom_call_target="tpu_custom_call" | custom-call | tf_op jit(solution)/shard_map/pallas_call | solution.py:449
  109.7 1.6 %copy.7 = f32[1,1,2,16,1536]{4,3,2,1,0:T(8,128)} copy(f32[1,1,2,16,1536]{4,3,2,1,0:T(8,128)} %bitcast.8) | data formatting | bytes 393216

commit v4 on v2

v4 whole, which is shorter than its diff:
```python
import functools

import jax
import jax.numpy as jnp
from jax import lax
from jax.experimental import pallas as pl
from jax.experimental.pallas import tpu as pltpu
from jax.sharding import PartitionSpec as P

MESH = pl.DeviceIdType.MESH
LANES = 128
STREAM_SLOTS = 6
LAST = 3
PIECES = 3
LOAD_SLOTS = 4
LOW_SCALE = 2.0**20
F8 = jnp.float8_e4m3fn
F32 = jnp.float32
BF16 = jnp.bfloat16
NN = (((1,), (0,)), ((), ()))
NT = (((1,), (1,)), ((), ()))


def kernel(
    ncol, nrow, nop, groups, pieces,
    real_hbm, imag_hbm, right_ref, upper_ref, src_ref, out_ref,
    src_all, right_all, upper_all, left_all, below_all, trace, inv,
    load_sem, isend, irecv, lsend, lrecv, usend, bsend, brecv,
):
    c = lax.axis_index("sx")
    r = lax.axis_index("sy")
    z = lax.axis_index("op")
    first = c + r == 0
    rows, width = real_hbm.shape
    srcs = src_ref.shape[1]
    group_rows = rows // groups
    split = group_rows // LANES
    piece = width // pieces
    blocks = rows // LANES
    ops = (real_hbm, imag_hbm)
    has_left, has_right = c > 0, c < ncol - 1
    has_below, has_above = r > 0, r < nrow - 1

    mate = 1 - r
    lower = r == 0

    def peer(j):
        return lax.rem(z + j, nop)

    def meet():
        barrier = pltpu.get_barrier_semaphore()

        def greet(cc, rr, zz):
            pl.semaphore_signal(barrier, inc=1, device_id=(cc, rr, zz), device_id_type=MESH)

        for j in range(nop):
            greet(c, mate, peer(j))
        for j in range(1, nop):
            greet(c, r, peer(j))
        for there, step in ((has_right, 1), (has_left, -1)):
            @pl.when(there)
            def _():
                for j in range(nop):
                    greet(c + step, r, peer(j))

        near = jnp.where(has_left, nop, 0) + jnp.where(has_right, nop, 0)
        pl.semaphore_wait(barrier, 2 * nop - 1 + near)
        src_all[z] = src_ref[...]
        right_all[z] = right_ref[...]
        upper_all[z] = upper_ref[...]

    def spread():
        for n in (2, 0, 1):
            for j in range(1, nop):
                fill(n, j).start()

    def fill(n, j):
        mine, whole = ((right_ref, right_all), (upper_ref, upper_all), (src_ref, src_all))[n]
        return pltpu.make_async_remote_copy(
            mine, whole.at[z], isend.at[n, j], irecv.at[n, j],
            device_id=(c, r, peer(j)), device_id_type=MESH,
        )

    def to_right(g, j):
        return pltpu.make_async_remote_copy(
            trace.at[g], left_all.at[z, g], lsend.at[g, j], lrecv.at[g, j],
            device_id=(c + 1, r, peer(j)), device_id_type=MESH,
        )

    def to_upper(g, j):
        return pltpu.make_async_remote_copy(
            trace.at[g], below_all.at[z, g], usend.at[g, j], brecv.at[g, j],
            device_id=(c, mate, peer(j)), device_id_type=MESH,
        )

    def along(g, j):
        return pltpu.make_async_remote_copy(
            left_all.at[z, g], left_all.at[z, g], bsend.at[g, j], lrecv.at[g, j],
            device_id=(c, r, peer(j)), device_id_type=MESH,
        )

    def span(g):
        return pl.ds(pl.multiple_of(g * group_rows, LANES), group_rows)

    def publish(g):
        @pl.when(has_right)
        def _():
            to_right(g, 0).start()

            @pl.when(has_below)
            def _():
                for j in range(1, nop):
                    to_right(g, j).start()

        @pl.when(lower)
        def _():
            for j in range(nop):
                to_upper(g, j).start()

        out_ref[:, :, span(g)] = trace[g]

    def take():
        @pl.when(jnp.logical_and(lower, has_left))
        def _():
            @pl.loop(0, groups)
            def _(g):
                to_right(g, 0).wait_recv()
                for j in range(1, nop):
                    along(g, j).start()

    def arrived(g):
        @pl.when(has_left)
        def _():
            for j in range(1, nop):
                to_right(g, j).wait_recv()

        @pl.when(has_below)
        def _():
            @pl.when(has_left)
            def _():
                to_right(g, 0).wait_recv()

            for j in range(nop):
                to_upper(g, j).wait_recv()

    def source(zz, g, h):
        cols = pl.ds(pl.multiple_of(g * group_rows + h * LANES, LANES), LANES)
        return [src_all[zz, k, :, cols] for k in range(2)]

    def incoming(zz, g, h):
        cols = pl.ds(pl.multiple_of(g * group_rows + h * LANES, LANES), LANES)
        lanes = slice(h * LANES, (h + 1) * LANES)
        value = source(zz, g, h)
        for coef, field in ((right_all, left_all), (upper_all, below_all)):
            cr, ci = coef[zz, 0:1, cols], coef[zz, 1:2, cols]
            fr, fi = field[zz, g, 0, :, lanes], field[zz, g, 1, :, lanes]
            value = [value[0] + (cr * fr - ci * fi), value[1] + (cr * fi + ci * fr)]
        return value

    def prepare(get, steps, slot, xw, x8, base):
        pairs = [get(zz, g, h) for zz, g in steps for h in range(split)]
        most = None
        for pair in pairs:
            both = jnp.maximum(jnp.abs(pair[0]), jnp.abs(pair[1]))
            most = both if most is None else jnp.maximum(most, both)
        top = jnp.maximum(jnp.max(most, axis=1, keepdims=True), 1e-30)
        scale = 256.0 / top
        back = top * (1.0 / (256.0 * LOW_SCALE))
        inv[slot] = jnp.broadcast_to(jnp.concatenate([back, back], axis=0), (2 * srcs, LANES))
        for n, pair in enumerate(pairs):
            for k in range(2):
                top_part = pair[k].astype(BF16)
                xw[base + n, k * srcs:(k + 1) * srcs, :] = top_part
                xw[base + n, (2 + k) * srcs:(3 + k) * srcs, :] = (
                    pair[k] - top_part.astype(F32)
                ).astype(BF16)
            x8[base + n] = jnp.concatenate([pair[0] * scale, pair[1] * scale], axis=0).astype(F8)

    def side(ref, base, count):
        return jnp.concatenate([ref[base + n] for n in range(count)], axis=1)

    def merge(big, small, slot):
        return big[:2 * srcs] + (big[2 * srcs:] + small * inv[slot][:, :1])

    def stream(stage, xw, x8):
        slots = stage.shape[0]
        seg = rows
        paired = (groups - 1) // 2 * 2
        early = nop * paired
        half = nop // 2
        chunks = early + 2 * half * (groups - paired)

        def units(i):
            k = lax.rem(i, 2)
            a, b = i // 2, (i - early) // 2
            in_pairs = i < early
            first_m = jnp.where(in_pairs, 2 * lax.rem(a, paired // 2), paired + b // half)
            first_j = jnp.where(in_pairs, a // (paired // 2), 2 * lax.rem(b, half))
            second_m = jnp.where(in_pairs, first_m + 1, first_m)
            second_j = jnp.where(in_pairs, first_j, first_j + 1)
            return k, ((first_m, first_j), (second_m, second_j))

        def hop(n):
            return jnp.where(lax.rem(n, 2) == 1, (n + 1) // 2, lax.rem(nop - n // 2, nop))

        def owner(n):
            return lax.rem(z - hop(n) + nop, nop)

        def load(i, u, op_k):
            _, pair = units(i)
            m, j = pair[u]
            slot = lax.rem(i, slots)
            return pltpu.make_async_copy(
                ops[op_k].at[
                    pl.ds(pl.multiple_of(m * group_rows, LANES), group_rows),
                    pl.ds(pl.multiple_of(owner(j) * seg, LANES), seg),
                ],
                stage.at[slot, u], load_sem.at[slot, u],
            )

        def fetch(i, op_k):
            for u in range(2):
                load(i, u, op_k).start()

        for i in range(slots):
            fetch(i, i % 2)
        meet()
        spread()
        trace[...] = jnp.zeros_like(trace)

        def chunk(i, op_k):
            _, pair = units(i)
            slot = lax.rem(i, slots)
            for u in range(2):
                load(i, u, op_k).wait()
            for u in range(2):
                m, j = pair[u]
                base = owner(j) * (groups * split)
                value = stage[slot, u]
                top_part = value.astype(BF16)
                rest = ((value - top_part.astype(F32)) * LOW_SCALE).astype(F8)
                big = lax.dot_general(side(xw, base, groups * split), top_part, NT, preferred_element_type=F32)
                small = lax.dot_general(side(x8, base, groups * split), rest, NT, preferred_element_type=F32)
                part = merge(big, small, j)
                if op_k == 0:
                    trace[m, 0] += part[:srcs]
                    trace[m, 1] += part[srcs:]
                else:
                    trace[m, 0] -= part[srcs:]
                    trace[m, 1] += part[:srcs]

            @pl.when(i + slots < chunks)
            def _():
                fetch(i + slots, op_k)

        @pl.loop(0, nop)
        def _(j):
            @pl.when(j > 0)
            def _():
                for n in range(3):
                    fill(n, hop(j)).wait_recv()

            steps = [(owner(j), g) for g in range(groups)]
            prepare(source, steps, j, xw, x8, owner(j) * (groups * split))

            @pl.loop(0, paired // 2)
            def _(a):
                for op_k in range(2):
                    chunk(2 * (j * (paired // 2) + a) + op_k, op_k)

        @pl.loop(0, paired)
        def _(m):
            publish(m)

        @pl.loop(0, groups - paired)
        def _(n):
            @pl.loop(0, half)
            def _(b):
                for op_k in range(2):
                    chunk(early + 2 * (n * half + b) + op_k, op_k)

            publish(paired + n)

    def resident(stage, high, low, xw, x8):
        slots = stage.shape[0]
        per = 2 * pieces
        chunks = per * blocks

        def load(i, n):
            k, p = n // pieces, n % pieces
            at = pl.multiple_of((i // per) * LANES, LANES)
            slot = lax.rem(i, slots)
            return pltpu.make_async_copy(
                ops[k].at[pl.ds(at, LANES), pl.ds(p * piece, piece)],
                stage.at[slot], load_sem.at[slot, 0],
            )

        for i in range(slots):
            load(i, i % per).start()
        meet()

        @pl.when(lower)
        def _():
            spread()


        @pl.when(jnp.logical_not(has_left))
        def _():
            left_all[...] = jnp.zeros_like(left_all)

        @pl.when(jnp.logical_not(has_below))
        def _():
            below_all[...] = jnp.zeros_like(below_all)

        @pl.loop(0, blocks)
        def _(blk):
            @pl.when(jnp.logical_and(has_below, blk == blocks // 2 - 1))
            def _():
                spread()

            for n in range(per):
                i = blk * per + n
                load(i, n).wait()
                value = stage[lax.rem(i, slots)].T
                top_part = value.astype(BF16)
                k, p = n // pieces, n % pieces
                cols = slice(p * piece, (p + 1) * piece)
                high[k, blk, cols, :] = top_part
                low[k, blk, cols, :] = ((value - top_part.astype(F32)) * LOW_SCALE).astype(F8)

                @pl.when(i + slots < chunks)
                def _():
                    load(i + slots, (n + slots) % per).start()

        trace[...] = jnp.zeros_like(trace)

        def weights(ref, k, m, g):
            tiles = []
            for zz in range(nop):
                at = pl.ds(pl.multiple_of(zz * rows + g * group_rows, LANES), group_rows)
                tiles.append(jnp.concatenate(
                    [ref[k, m * split + h, at, :] for h in range(split)], axis=1
                ))
            return jnp.concatenate(tiles, axis=0)

        count = nop * split

        def multiply(m, pairs):
            wide = jnp.concatenate([side(xw, slot * count, count) for _, slot in pairs], axis=1)
            parts = []
            for k in range(2):
                tall = jnp.concatenate([weights(high, k, m, g) for g, _ in pairs], axis=0)
                part = lax.dot_general(wide, tall, NN, preferred_element_type=F32)
                part = part[:2 * srcs], part[2 * srcs:]
                for g, slot in pairs:
                    small = lax.dot_general(
                        side(x8, slot * count, count), weights(low, k, m, g), NN,
                        preferred_element_type=F32,
                    )
                    part = part[0], part[1] + small * inv[slot][:, :1]
                parts.append(part[0] + part[1])
            trace[m, 0] += parts[0][:srcs] - parts[1][srcs:]
            trace[m, 1] += parts[1][:srcs] + parts[0][srcs:]

        last = min(LAST, groups)
        early = groups - last

        def ready(g, slot):
            arrived(g)
            prepare(incoming, [(zz, g) for zz in range(nop)], slot, xw, x8, slot * count)

        for n in range(3):
            for j in range(1, nop):
                fill(n, j).wait_recv()
        take()

        @pl.loop(0, early)
        def _(g):
            ready(g, 0)
            for m in range(groups):
                multiply(m, [(g, 0)])

        for n in range(last):
            ready(early + n, n)

        @pl.loop(0, groups)
        def _(m):
            multiply(m, [(early + n, n) for n in range(last)])
            publish(m)

    @pl.when(first)
    def _():
        pl.run_scoped(
            stream,
            pltpu.VMEM((STREAM_SLOTS, 2, group_rows, rows), F32),
            pltpu.VMEM((width // LANES, 4 * srcs, LANES), BF16),
            pltpu.VMEM((width // LANES, 2 * srcs, LANES), F8),
        )

    @pl.when(jnp.logical_not(first))
    def _():
        pl.run_scoped(
            resident,
            pltpu.VMEM((LOAD_SLOTS, LANES, piece), F32),
            pltpu.VMEM((2, blocks, width, LANES), BF16),
            pltpu.VMEM((2, blocks, width, LANES), F8),
            pltpu.VMEM((min(LAST, groups) * nop * split, 4 * srcs, LANES), BF16),
            pltpu.VMEM((min(LAST, groups) * nop * split, 2 * srcs, LANES), F8),
        )

    for n in range(3):
        for j in range(1, nop):
            fill(n, j).wait_send()

    @pl.loop(0, groups)
    def _(g):
        @pl.when(has_right)
        def _():
            to_right(g, 0).wait_send()

            @pl.when(has_below)
            def _():
                for j in range(1, nop):
                    to_right(g, j).wait_send()

        @pl.when(lower)
        def _():
            for j in range(nop):
                to_upper(g, j).wait_send()

            @pl.when(has_left)
            def _():
                for j in range(1, nop):
                    along(g, j).wait_send()


def solution(mesh):
    ncol, nrow, nop = (mesh.shape[a] for a in ("sx", "sy", "op"))

    def shards(op_real, op_imag, coef_right, coef_upper, sources):
        rows, width = op_real.shape[2:]
        srcs = sources.shape[3]
        groups = rows // 256 if rows % 256 == 0 else rows // 128
        group_rows = rows // groups
        pieces = PIECES if width % (PIECES * LANES) == 0 else 1
        vmem = pl.BlockSpec(memory_space=pltpu.VMEM)
        hbm = pl.BlockSpec(memory_space=pl.ANY)
        dma = pltpu.SemaphoreType.DMA
        out = pl.pallas_call(
            functools.partial(kernel, ncol, nrow, nop, groups, pieces),
            out_shape=jax.ShapeDtypeStruct((2, srcs, rows), F32),
            in_specs=[hbm, hbm, vmem, vmem, vmem],
            out_specs=vmem,
            scratch_shapes=[
                pltpu.VMEM((nop, 2, srcs, rows), F32),
                pltpu.VMEM((nop, 2, rows), F32),
                pltpu.VMEM((nop, 2, rows), F32),
                pltpu.VMEM((nop, groups, 2, srcs, group_rows), F32),
                pltpu.VMEM((nop, groups, 2, srcs, group_rows), F32),
                pltpu.VMEM((groups, 2, srcs, group_rows), F32),
                pltpu.VMEM((max(LAST, nop), 2 * srcs, LANES), F32),
                dma((max(STREAM_SLOTS, LOAD_SLOTS), 2)),
                dma((3, nop)),
                dma((3, nop)),
                dma((groups, nop)),
                dma((groups, nop)),
                dma((groups, nop)),
                dma((groups, nop)),
                dma((groups, nop)),
            ],
            compiler_params=pltpu.CompilerParams(
                collective_id=0, has_side_effects=True, vmem_limit_bytes=67043328
            ),
        )(op_real[0, 0], op_imag[0, 0], coef_right[0, 0], coef_upper[0, 0], sources[0, 0])
        return out[None, None]

    return jax.shard_map(
        shards,
        mesh=mesh,
        in_specs=(
            P("sx", "sy", "op", None),
            P("sx", "sy", "op", None),
            P("sx", "sy", None, "op"),
            P("sx", "sy", None, "op"),
            P("sx", "sy", None, None, "op"),
        ),
        out_specs=P("sx", "sy", None, None, "op"),
        check_vma=False,
    )
```

time: 102 us -> 97.5 us (0.956)
  Pallas kernels: 101 us -> 95.7 us
    pallas_call x1, Pallas kernels: 101 us -> 95.7 us  [shards(): pl.pallas_call(functools.partial(kernel, ncol, nrow, nop, groups, pieces)...]
where the time goes in v4:
time: 97.5 us; the launch traced here: 97.3 us
  Pallas kernels  95.7 us (98%)
  local copies, waits for them, and re-layouts  1.62 us (2%)
    pallas_call x1, Pallas kernels, shards(): pl.pallas_call(functools.partial(kernel, ncol, nrow, nop, groups, pieces)...  95.7 us

profile of v4, /device:TPU:7, one launch (start us, length us, event | category | flops | bytes accessed | tf_op | source)
XLA Modules:
  0.0 97.3 jit_solution(8870208327546953783)
XLA Ops:
  0.0 95.7 %shard_map.55 = f32[2,16,1536]{2,1,0:T(8,128)} custom-call(f32[1536,6144]{1,0:T(8,128)} %bitcast.6, f32[1536,6144]{1,0:T(8,128)} %bitcast.7, f32[2,1536]{1,0:T(2,128)} %bitcast.10, f32[2,1536]{1,0:T(2,128)} %bitcast.11, f32[2,16,1536]{2,1,0:T(8,128)} %bitcast.9), custom_call_target="tpu_custom_call" | custom-call | tf_op jit(solution)/shard_map/pallas_call | solution.py:449
  95.7 1.6 %copy.7 = f32[1,1,2,16,1536]{4,3,2,1,0:T(8,128)} copy(f32[1,1,2,16,1536]{4,3,2,1,0:T(8,128)} %bitcast.8) | data formatting | bytes 393216

commit v5 on v4

--- a/solution.py
+++ b/solution.py
@@ -9,7 +9,7 @@
 
 MESH = pl.DeviceIdType.MESH
 LANES = 128
-STREAM_SLOTS = 6
+STREAM_SLOTS = 8
 LAST = 3
 PIECES = 3
 LOAD_SLOTS = 4
@@ -25,7 +25,7 @@
     ncol, nrow, nop, groups, pieces,
     real_hbm, imag_hbm, right_ref, upper_ref, src_ref, out_ref,
     src_all, right_all, upper_all, left_all, below_all, trace, inv,
-    load_sem, isend, irecv, lsend, lrecv, usend, bsend, brecv,
+    load_sem, isend, irecv, lsend, lrecv, usend, bsend, brecv, relay, rrecv,
 ):
     c = lax.axis_index("sx")
     r = lax.axis_index("sy")
@@ -63,7 +63,23 @@
                 for j in range(nop):
                     greet(c + step, r, peer(j))
 
+        @pl.when(lends)
+        def _():
+            greet(served, mate, z)
+
+        @pl.when(relays)
+        def _():
+            greet(served, mate, z)
+            for j in range(nop):
+                greet(served + 1, mate, peer(j))
+
+        @pl.when(gets)
+        def _():
+            for j in range(nop):
+                greet(lax.rem(c + 1, 4), mate, peer(j))
+
         near = jnp.where(has_left, nop, 0) + jnp.where(has_right, nop, 0)
+        near += jnp.where(lends, 1, 0) + jnp.where(relays, nop + 1, 0) + jnp.where(gets, nop, 0)
         pl.semaphore_wait(barrier, 2 * nop - 1 + near)
         src_all[z] = src_ref[...]
         right_all[z] = right_ref[...]
@@ -93,6 +109,47 @@
             device_id=(c, mate, peer(j)), device_id_type=MESH,
         )
 
+    detour = ncol == 4
+    late = (groups - 1) // 2 * 2
+    served = lax.rem(c + 2, 4)
+    lends = jnp.logical_and(jnp.logical_and(lower, detour), jnp.logical_and(c > 0, has_right))
+    relays = jnp.logical_and(
+        jnp.logical_and(has_below, detour), jnp.logical_and(served > 0, served < ncol - 1)
+    )
+    gets = jnp.logical_and(jnp.logical_and(lower, detour), c > 1)
+
+    def straight(g):
+        return jnp.logical_or(has_below, jnp.logical_and(c == 0, g < late))
+
+    def lent(g):
+        return jnp.logical_and(lends, lax.rem(g, 2) == 0)
+
+    def spreads(g):
+        own = jnp.logical_or(c > 1, jnp.logical_and(c == 1, g >= late))
+        direct = jnp.logical_and(gets, lax.rem(g, 2) == 0)
+        return jnp.logical_and(jnp.logical_and(lower, own), jnp.logical_not(direct))
+
+    def lend(g):
+        return pltpu.make_async_remote_copy(
+            trace.at[g], relay.at[g], lsend.at[g, 0], rrecv.at[g],
+            device_id=(lax.rem(c + 2, 4), mate, z), device_id_type=MESH,
+        )
+
+    def pass_on(g, j):
+        return pltpu.make_async_remote_copy(
+            relay.at[g], left_all.at[z, g], bsend.at[g, j], lrecv.at[g, j],
+            device_id=(served + 1, mate, peer(j)), device_id_type=MESH,
+        )
+
+    def serve(when):
+        @pl.when(jnp.logical_and(relays, when))
+        def _():
+            @pl.loop(0, (groups + 1) // 2)
+            def _(n):
+                lend(2 * n).wait_recv()
+                for j in range(nop):
+                    pass_on(2 * n, j).start()
+
     def along(g, j):
         return pltpu.make_async_remote_copy(
             left_all.at[z, g], left_all.at[z, g], bsend.at[g, j], lrecv.at[g, j],
@@ -105,9 +162,15 @@
     def publish(g):
         @pl.when(has_right)
         def _():
-            to_right(g, 0).start()
-
-            @pl.when(has_below)
+            @pl.when(lent(g))
+            def _():
+                lend(g).start()
+
+            @pl.when(jnp.logical_not(lent(g)))
+            def _():
+                to_right(g, 0).start()
+
+            @pl.when(straight(g))
             def _():
                 for j in range(1, nop):
                     to_right(g, j).start()
@@ -120,10 +183,10 @@
         out_ref[:, :, span(g)] = trace[g]
 
     def take():
-        @pl.when(jnp.logical_and(lower, has_left))
-        def _():
-            @pl.loop(0, groups)
-            def _(g):
+        @pl.loop(0, groups)
+        def _(g):
+            @pl.when(spreads(g))
+            def _():
                 to_right(g, 0).wait_recv()
                 for j in range(1, nop):
                     along(g, j).start()
@@ -134,12 +197,12 @@
             for j in range(1, nop):
                 to_right(g, j).wait_recv()
 
+            @pl.when(jnp.logical_not(spreads(g)))
+            def _():
+                to_right(g, 0).wait_recv()
+
         @pl.when(has_below)
         def _():
-            @pl.when(has_left)
-            def _():
-                to_right(g, 0).wait_recv()
-
             for j in range(nop):
                 to_upper(g, j).wait_recv()
 
@@ -201,7 +264,7 @@
             return k, ((first_m, first_j), (second_m, second_j))
 
         def hop(n):
-            return jnp.where(lax.rem(n, 2) == 1, (n + 1) // 2, lax.rem(nop - n // 2, nop))
+            return n
 
         def owner(n):
             return lax.rem(z - hop(n) + nop, nop)
@@ -372,6 +435,7 @@
         for n in range(3):
             for j in range(1, nop):
                 fill(n, j).wait_recv()
+        serve(c > served)
         take()
 
         @pl.loop(0, early)
@@ -387,6 +451,8 @@
         def _(m):
             multiply(m, [(early + n, n) for n in range(last)])
             publish(m)
+
+        serve(c < served)
 
     @pl.when(first)
     def _():
@@ -418,7 +484,7 @@
         def _():
             to_right(g, 0).wait_send()
 
-            @pl.when(has_below)
+            @pl.when(straight(g))
             def _():
                 for j in range(1, nop):
                     to_right(g, j).wait_send()
@@ -428,10 +494,15 @@
             for j in range(nop):
                 to_upper(g, j).wait_send()
 
-            @pl.when(has_left)
-            def _():
-                for j in range(1, nop):
-                    along(g, j).wait_send()
+        @pl.when(spreads(g))
+        def _():
+            for j in range(1, nop):
+                along(g, j).wait_send()
+
+        @pl.when(jnp.logical_and(relays, lax.rem(g, 2) == 0))
+        def _():
+            for j in range(nop):
+                pass_on(g, j).wait_send()
 
 
 def solution(mesh):
@@ -467,6 +538,8 @@
                 dma((groups, nop)),
                 dma((groups, nop)),
                 dma((groups, nop)),
+                pltpu.VMEM((groups, 2, srcs, group_rows), F32),
+                dma((groups,)),
             ],
             compiler_params=pltpu.CompilerParams(
                 collective_id=0, has_side_effects=True, vmem_limit_bytes=67043328

time: 97.5 us -> 93.2 us (0.956)
  Pallas kernels: 95.7 us -> 91.4 us
    pallas_call x1, Pallas kernels: 95.7 us -> 91.4 us  [shards(): pl.pallas_call(functools.partial(kernel, ncol, nrow, nop, groups, pieces)...]
where the time goes in v5:
time: 93.2 us; the launch traced here: 93 us
  Pallas kernels  91.4 us (98%)
  local copies, waits for them, and re-layouts  1.62 us (2%)
    pallas_call x1, Pallas kernels, shards(): pl.pallas_call(functools.partial(kernel, ncol, nrow, nop, groups, pieces)...  91.4 us

profile of v5, /device:TPU:7, one launch (start us, length us, event | category | flops | bytes accessed | tf_op | source)
XLA Modules:
  0.0 93.0 jit_solution(2438648573400213954)
XLA Ops:
  0.0 91.4 %shard_map.55 = f32[2,16,1536]{2,1,0:T(8,128)} custom-call(f32[1536,6144]{1,0:T(8,128)} %bitcast.6, f32[1536,6144]{1,0:T(8,128)} %bitcast.7, f32[2,1536]{1,0:T(2,128)} %bitcast.10, f32[2,1536]{1,0:T(2,128)} %bitcast.11, f32[2,16,1536]{2,1,0:T(8,128)} %bitcast.9), custom_call_target="tpu_custom_call" | custom-call | tf_op jit(solution)/shard_map/pallas_call | solution.py:520
  91.4 1.6 %copy.7 = f32[1,1,2,16,1536]{4,3,2,1,0:T(8,128)} copy(f32[1,1,2,16,1536]{4,3,2,1,0:T(8,128)} %bitcast.8) | data formatting | bytes 393216

commit v6 on v5

--- a/solution.py
+++ b/solution.py
@@ -248,7 +248,7 @@
     def stream(stage, xw, x8):
         slots = stage.shape[0]
         seg = rows
-        paired = (groups - 1) // 2 * 2
+        paired = groups // 2 * 2
         early = nop * paired
         half = nop // 2
         chunks = early + 2 * half * (groups - paired)
@@ -331,9 +331,10 @@
                 for op_k in range(2):
                     chunk(2 * (j * (paired // 2) + a) + op_k, op_k)
 
-        @pl.loop(0, paired)
-        def _(m):
-            publish(m)
+                @pl.when(j == nop - 1)
+                def _():
+                    publish(2 * a)
+                    publish(2 * a + 1)
 
         @pl.loop(0, groups - paired)
         def _(n):
@@ -377,7 +378,7 @@
 
         @pl.loop(0, blocks)
         def _(blk):
-            @pl.when(jnp.logical_and(has_below, blk == blocks // 2 - 1))
+            @pl.when(jnp.logical_and(has_below, blk == jnp.where(c == 0, blocks // 3, blocks // 2 - 1)))
             def _():
                 spread()
 

time: 93.2 us -> 92.3 us (level)
  no operation moved by 1% of the time
where the time goes in v6:
time: 92.3 us; the launch traced here: 92.2 us
  Pallas kernels  90.6 us (98%)
  local copies, waits for them, and re-layouts  1.62 us (2%)
    pallas_call x1, Pallas kernels, shards(): pl.pallas_call(functools.partial(kernel, ncol, nrow, nop, groups, pieces)...  90.6 us

profile of v6, /device:TPU:7, one launch (start us, length us, event | category | flops | bytes accessed | tf_op | source)
XLA Modules:
  0.0 92.2 jit_solution(9771642344340163289)
XLA Ops:
  0.0 90.6 %shard_map.55 = f32[2,16,1536]{2,1,0:T(8,128)} custom-call(f32[1536,6144]{1,0:T(8,128)} %bitcast.6, f32[1536,6144]{1,0:T(8,128)} %bitcast.7, f32[2,1536]{1,0:T(2,128)} %bitcast.10, f32[2,1536]{1,0:T(2,128)} %bitcast.11, f32[2,16,1536]{2,1,0:T(8,128)} %bitcast.9), custom_call_target="tpu_custom_call" | custom-call | tf_op jit(solution)/shard_map/pallas_call | solution.py:521
  90.6 1.6 %copy.7 = f32[1,1,2,16,1536]{4,3,2,1,0:T(8,128)} copy(f32[1,1,2,16,1536]{4,3,2,1,0:T(8,128)} %bitcast.8) | data formatting | bytes 393216

commit v7 on v6

--- a/solution.py
+++ b/solution.py
@@ -12,7 +12,7 @@
 STREAM_SLOTS = 8
 LAST = 3
 PIECES = 3
-LOAD_SLOTS = 4
+LOAD_SLOTS = 5
 LOW_SCALE = 2.0**20
 F8 = jnp.float8_e4m3fn
 F32 = jnp.float32

time: 92.3 us -> 92.2 us (level)
  no operation moved by 1% of the time
where the time goes in v7:
time: 92.2 us; the launch traced here: 92.1 us
  Pallas kernels  90.5 us (98%)
  local copies, waits for them, and re-layouts  1.62 us (2%)
    pallas_call x1, Pallas kernels, shards(): pl.pallas_call(functools.partial(kernel, ncol, nrow, nop, groups, pieces)...  90.5 us

profile of v7, /device:TPU:7, one launch (start us, length us, event | category | flops | bytes accessed | tf_op | source)
XLA Modules:
  0.0 92.1 jit_solution(10241856554105440267)
XLA Ops:
  0.0 90.5 %shard_map.55 = f32[2,16,1536]{2,1,0:T(8,128)} custom-call(f32[1536,6144]{1,0:T(8,128)} %bitcast.6, f32[1536,6144]{1,0:T(8,128)} %bitcast.7, f32[2,1536]{1,0:T(2,128)} %bitcast.10, f32[2,1536]{1,0:T(2,128)} %bitcast.11, f32[2,16,1536]{2,1,0:T(8,128)} %bitcast.9), custom_call_target="tpu_custom_call" | custom-call | tf_op jit(solution)/shard_map/pallas_call | solution.py:521
  90.5 1.6 %copy.7 = f32[1,1,2,16,1536]{4,3,2,1,0:T(8,128)} copy(f32[1,1,2,16,1536]{4,3,2,1,0:T(8,128)} %bitcast.8) | data formatting | bytes 393216
